TPU v7x, 256 devices: a whole 4x4x8 slice. The times are simulated.
256 devices in a mesh: row: 32 (over x, z_hi, core), col: 8 (over y, z_lo).
Axes of the slice: x: 4, y: 4, z: 8 (z_hi: 4, z_lo: 2; z = z_hi * 2 + z_lo), core: 2. Of those that a mesh axis runs over, the one named last changes fastest.
Arguments:
- ancestor_inverse: bfloat16 [24576, 8, 3072], P('row', 'col'), may hold values from -6 to 6
- parent_panel: bfloat16 [24576, 1024], P(('row', 'col')), may hold values from -0.15625 to 0.15625
- parent_diag_inv: bfloat16 [1024, 1024], replicated, may hold values from -1.5 to 1.5, as said below
- child_panel_anc: bfloat16 [24576, 1024], P(('row', 'col')), may hold values from -0.15625 to 0.15625
- child_panel_par: bfloat16 [1024, 1024], replicated, may hold values from -0.1875 to 0.1875
- child_diag_inv: bfloat16 [1024, 1024], replicated, may hold values from -1.5 to 1.5, as said below
Outputs:
- ainv_ap: float32 [24576, 1024], P(('row', 'col'))
- ainv_pp: float32 [1024, 1024], P(('row', 'col'))
- ainv_ac: float32 [24576, 1024], P(('row', 'col'))
- ainv_pc: float32 [1024, 1024], P(('row', 'col'))
- ainv_cc: float32 [1024, 1024], P(('row', 'col'))
Inputs may be any that keep to these rules, and one draw needn't show every extreme that they name: `parent_diag_inv`: lower triangular, with diagonal entries between 0.5 and 1.5. `child_diag_inv`: lower triangular, with diagonal entries between 0.5 and 1.5.
All inputs are finite; a program needn't handle non-finite values.
Results may differ from a plain program's by a relative error of at most 0.0041.
Values may be sent and summed in bfloat16 or wider, within the bound.
No kernel may reach another device: no remote copies, remote signals or barrier semaphores. Data moves between devices by JAX's collectives and lax.ppermute only.
A program may use at most 128 MiB of HBM per device.

v0:
```python
import jax
import jax.numpy as jnp
from jax import lax
from jax.sharding import Mesh, PartitionSpec as P

ROW = ("x", "zh", "core")
COL = ("y", "zl")
ALL = ROW + COL
BF = jnp.bfloat16
F32 = jnp.float32


def dot(a, b, ca=1, cb=0):
    return lax.dot_general(a, b, (((ca,), (cb,)), ((), ())), preferred_element_type=F32)


def shards(z, pp, pdi, ca, cp, cdi):
    rows, w = pp.shape
    nr, nc = (lax.axis_size(ROW), lax.axis_size(COL))
    sl = w // nr
    mine = sl // nc
    block = z.reshape(z.shape[0], -1)
    panels = lax.all_gather(jnp.concatenate([pp, ca], axis=1), ROW, axis=0, tiled=True)
    part = dot(block, panels).astype(BF).reshape(nc, rows, 2 * w)
    got = lax.all_to_all(part, COL, 0, 0, tiled=True)
    total = jnp.sum(got.astype(F32), axis=0)
    upper, lower = (total[:, :w], total[:, w:])
    u = upper.astype(BF)
    shifted = dot(u, cp)
    s = shifted.astype(BF)
    anc = lower - shifted
    a = anc.astype(BF)
    x = jnp.stack([u.T, s.T, a.T]).reshape(3, nr, sl, rows).transpose(1, 0, 2, 3)
    x = lax.all_to_all(x, ROW, 0, 0, tiled=True)
    x = x.transpose(1, 2, 0, 3).reshape(3 * sl, nr * rows)
    g = dot(x, panels)
    g1t = g[:sl, :w]
    cross = g[:sl, w:]
    stp = g[sl : 2 * sl, :w]
    stc = g[sl : 2 * sl, w:]
    atc = g[2 * sl :, w:]
    t2 = dot(stp.astype(BF), cp) + atc
    t = jnp.stack([g1t, t2]).reshape(2, sl, nr, sl).transpose(2, 0, 3, 1)
    t = lax.all_to_all(t, ROW, 0, 0, tiled=True)
    t = t.transpose(1, 2, 0, 3).reshape(2, sl, w)
    f = jnp.stack([t[0], cross, t[1] - stc]).reshape(3, nc, mine, w).transpose(1, 0, 2, 3)
    f = lax.all_to_all(f, COL, 0, 0, tiled=True)
    f = jnp.sum(f, axis=0)
    diag_prod = dot(pdi, cp).astype(BF)
    first = (lax.axis_index(ROW) * nc + lax.axis_index(COL)) * mine
    cols = lambda m: lax.dynamic_slice_in_dim(m, first, mine, 1)
    pp_out = dot(cols(pdi), pdi, 0, 0) + f[0]
    pc = f[1] - dot(pp_out.astype(BF), cp)
    cc = dot(cols(cdi), cdi, 0, 0) + dot(cols(diag_prod), diag_prod, 0, 0) + f[2]
    return (-upper, pp_out, -anc, pc, cc)


def solution(mesh):
    fine = Mesh(mesh.devices.reshape(4, 4, 2, 4, 2), ALL)
    out = P(ALL, None)
    return jax.shard_map(
        shards,
        mesh=fine,
        in_specs=(P(ROW, COL, None), out, P(), out, P(), P()),
        out_specs=(out,) * 5,
        check_vma=False,
    )
```

profile of v0, /device:TPU:1, one launch (start us, length us, event | category | flops | bytes accessed | tf_op | source)
XLA Modules:
  0.0 265.3 jit_solution(7984998674487563898)
XLA Ops:
  7.2 0.0 copy-start
  7.2 0.0 all-gather.2.cloned.1.call-start
  7.2 1.9 pad_maximum_fusion
  9.2 0.0 all-gather.2.cloned.1.call-update
  9.2 98.4 %all-gather.2.cloned.1.call-done = bf16[3072,2048]{1,0:T(8,128)(2,1)} async-done(((bf16[96,2048]{1,0:T(8,128)(2,1)}), bf16[3072,2048]{1,0:T(8,128)(2,1)}) %all-gather.2.cloned.1.call-update) | async-done | bytes 12582928 | tf_op jit(solution)/shard_map/all_gather | solution.py:23
  107.6 14.3 %fusion.2 = bf16[2048,768]{0,1:T(8,128)(2,1)S(1)} fusion(bf16[3072,2048]{1,0:T(8,128)(2,1)} %all-gather.2.cloned.1.call-done, bf16[768,1,3072]{2,0,1:T(8,128)(2,1)} %param.6), kind=kOutput, calls=%fused_computation.3 | convolution fusion | flops 9665249280 | bytes 20447232 | tf_op jit(solution)/shard_map/dot_general | solution.py:14
  121.8 47.8 %all_to_all.20 = bf16[8,96,2048]{2,1,0:T(8,128)(2,1)S(1)} all-to-all(bf16[8,96,2048]{2,1,0:T(8,128)(2,1)S(1)} %bitcast.57), channel_id=1, replica_groups=mesh['x'=4,'zh'=4,'core'=2,'y'=4,'zl'=2] {'y','zl'}, dimensions={0} | all-to-all | bytes 6291456 | tf_op jit(solution)/shard_map/all_to_all | solution.py:25
  169.7 0.6 convert_reduce_fusion
  170.3 0.0 copy-done
  170.3 1.3 fusion.9
  171.5 0.2 copy.30
  171.7 0.2 copy.31
  171.9 0.2 copy.29
  172.1 0.2 maximum_bitcast_fusion.1
  172.3 0.1 copy.32
  172.3 31.4 %all_to_all.21 = bf16[32,3,32,96]{3,2,1,0:T(8,128)(2,1)S(1)} all-to-all(bf16[32,3,32,96]{3,2,1,0:T(8,128)(2,1)S(1)} %copy.32), channel_id=1, replica_groups=mesh['x'=4,'zh'=4,'core'=2,'y'=4,'zl'=2] {'x','zh','core'}, dimensions={0} | all-to-all | bytes 1179648 | tf_op jit(solution)/shard_map/all_to_all | solution.py:34
  203.7 0.3 copy.33
  204.1 1.1 reshape.44
  205.1 6.7 %fusion.19 = f32[96,2048]{1,0:T(8,128)S(1)} fusion(bf16[96,3072]{1,0:T(8,128)(2,1)S(1)} %reshape.44, bf16[3072,2048]{1,0:T(8,128)(2,1)} %all-gather.2.cloned.1.call-done), kind=kOutput, calls=%fused_computation.37 | convolution fusion | flops 1207959552 | bytes 13959168 | tf_op jit(solution)/shard_map/dot_general | solution.py:14
  211.8 0.9 copy-done.1
  212.7 0.5 convolution_add_fusion
  213.1 1.0 copy.39
  214.2 1.0 copy.40
  215.2 1.3 maximum_bitcast_fusion
  216.5 1.1 reshape.45
  217.6 5.5 %all-to-all-start.2 = ((f32[32,1,2048]{2,1,0:T(1,128)}), f32[32,1,2048]{2,1,0:T(1,128)S(1)}, u32[]{:S(2)}, u32[]{:S(2)}) async-start(f32[32,1,2048]{2,1,0:T(1,128)} %reshape.45), calls=%async_computation.2 | async-start | bytes 524288 | tf_op jit(solution)/shard_map/all_to_all | solution.py:44
  223.1 12.9 %all-to-all-done.2 = f32[32,1,2048]{2,1,0:T(1,128)S(1)} async-done(((f32[32,1,2048]{2,1,0:T(1,128)}), f32[32,1,2048]{2,1,0:T(1,128)S(1)}, u32[]{:S(2)}, u32[]{:S(2)}) %all-to-all-start.2) | async-done | bytes 262176 | tf_op jit(solution)/shard_map/all_to_all | solution.py:44
  236.0 0.5 broadcast
  236.5 1.3 reduce
  237.8 0.3 reshape.46
  238.1 0.9 fusion.17
  239.0 0.3 copy.37
  239.3 0.2 squeeze.12
  239.6 1.0 fusion.18
  240.7 0.3 copy.36
  241.0 0.3 stack.39
  241.3 0.1 maximum_bitcast_fusion.2
  241.4 0.8 copy.38
  242.1 3.5 %all-to-all-start.3 = ((f32[8,3,4,1024]{3,2,1,0:T(4,128)}), f32[8,3,4,1024]{3,2,1,0:T(4,128)S(1)}, u32[]{:S(2)}, u32[]{:S(2)}) async-start(f32[8,3,4,1024]{3,2,1,0:T(4,128)} %copy.38), calls=%async_computation.3 | async-start | bytes 786432 | tf_op jit(solution)/shard_map/all_to_all | solution.py:47
  245.6 0.0 copy-start.2
  245.6 2.3 fusion.6
  247.9 3.7 %convolution_convert_fusion = bf16[1024,1024]{0,1:T(8,128)(2,1)} fusion(bf16[1024,1024]{1,0:T(8,128)(2,1)S(1)} %copy-done.2, bf16[1024,1024]{1,0:T(8,128)(2,1)S(1)} %copy-done), kind=kOutput, calls=%fused_computation.4 | convolution fusion | flops 2148532224 | bytes 6291456 | tf_op jit(solution)/shard_map/dot_general | solution.py:14
  251.7 2.1 all-to-all-done.3
  253.8 0.1 reduce_sum.19
  253.9 2.3 convolution_add_fusion.2
  256.2 1.0 convolution_subtract_fusion
  257.2 0.0 copy-done.3
  257.2 1.3 fusion.5
  (11 shorter events, 0.1 us)
Async XLA Ops:
  7.2 163.1 %copy-start = (bf16[1024,1024]{1,0:T(8,128)(2,1)S(1)}, bf16[1024,1024]{1,0:T(8,128)(2,1)}, u32[]{:S(2)}) copy-start(bf16[1024,1024]{1,0:T(8,128)(2,1)} %param.10) | copy-start | bytes 6291460
  7.2 100.4 %all-gather.2.cloned.1.call-start = ((), (), s32[]{:S(2)}) async-start(), calls=%async_computation.4 | async-start | bytes 12976128 | tf_op jit(solution)/shard_map/all_gather | solution.py:23
  211.8 0.9 copy-start.1
  217.6 18.4 %all-to-all-start.2 = ((f32[32,1,2048]{2,1,0:T(1,128)}), f32[32,1,2048]{2,1,0:T(1,128)S(1)}, u32[]{:S(2)}, u32[]{:S(2)}) async-start(f32[32,1,2048]{2,1,0:T(1,128)} %reshape.45), calls=%async_computation.2 | async-start | bytes 524288 | tf_op jit(solution)/shard_map/all_to_all | solution.py:44
  239.0 1.6 copy-start.4
  242.1 11.7 %all-to-all-start.3 = ((f32[8,3,4,1024]{3,2,1,0:T(4,128)}), f32[8,3,4,1024]{3,2,1,0:T(4,128)S(1)}, u32[]{:S(2)}, u32[]{:S(2)}) async-start(f32[8,3,4,1024]{3,2,1,0:T(4,128)} %copy.38), calls=%async_computation.3 | async-start | bytes 786432 | tf_op jit(solution)/shard_map/all_to_all | solution.py:47
  245.6 2.3 copy-start.2
  253.9 3.3 %copy-start.3 = (bf16[1024,1024]{0,1:T(8,128)(2,1)S(1)}, bf16[1024,1024]{0,1:T(8,128)(2,1)}, u32[]{:S(2)}) copy-start(bf16[1024,1024]{0,1:T(8,128)(2,1)} %convolution_convert_fusion) | copy-start | bytes 6291460
  256.2 2.3 copy-start.5
Sparse Core Ops, SparseCore 0:
  11.1 96.4 all-gather.1
where the time goes:
time: 266 us; the launch traced here: 265 us
  waiting for transfers between devices  113 us (42%)
  blocking collectives  79.2 us (30%)
  matrix products  33.3 us (13%)
  between operations  14.3 us (5%)
  local copies, waits for them, and re-layouts  9.7 us (4%)
  starting transfers between devices  8.97 us (3%)
  other arithmetic  6.4 us (2%)
    all_gather x1, waiting for transfers between devices, shards(): lax.all_gather(jnp.concatenate([pp, ca], axis=1), ROW, axis=0, tiled=True)  98.4 us
    all_to_all x1, blocking collectives, shards(): got = lax.all_to_all(part, COL, 0, 0, tiled=True)  47.8 us
    dot_general x9, matrix products, dot(): lax.dot_general(a, b, (((ca,), (cb,)), ((), ())), preferred_element_type=...  33.3 us
    all_to_all x1, blocking collectives, shards(): x = lax.all_to_all(x, ROW, 0, 0, tiled=True)  31.4 us
    all_to_all x1, waiting for transfers between devices, shards(): t = lax.all_to_all(t, ROW, 0, 0, tiled=True)  12.9 us
    all_to_all x1, starting transfers between devices, shards(): t = lax.all_to_all(t, ROW, 0, 0, tiled=True)  5.48 us
  transfers between devices with their start and end apart: 3, of which 3 were waited for; matrix products, arithmetic and copies ran while one was open for 2% of the time, Pallas kernels for 0%

commit v1 on v0

--- a/solution.py
+++ b/solution.py
@@ -20,7 +20,12 @@
     sl = w // nr
     mine = sl // nc
     block = z.reshape(z.shape[0], -1)
-    panels = lax.all_gather(jnp.concatenate([pp, ca], axis=1), ROW, axis=0, tiled=True)
+    panels = jnp.concatenate(
+        lax.all_to_all(
+            jnp.stack([jnp.concatenate([pp, ca], axis=1)] * lax.axis_size(ROW)), ROW, 0, 0
+        ),
+        axis=0,
+    )
     part = dot(block, panels).astype(BF).reshape(nc, rows, 2 * w)
     got = lax.all_to_all(part, COL, 0, 0, tiled=True)
     total = jnp.sum(got.astype(F32), axis=0)

time: 266 us -> 437 us (1.64)
  blocking collectives: 79.2 us -> 361 us
  waiting for transfers between devices: 113 us -> 14.8 us
  between operations: 14.3 us -> 0.88 us
  local copies, waits for them, and re-layouts: 9.7 us -> 15.9 us
    all_to_all x0 -> x1, blocking collectives: none -> 289 us  [shards(): lax.all_to_all(jnp.stack([jnp.concatenate([pp, ca], axis=1)] * lax.axis_s...]
    all_gather x1 -> x0, waiting for transfers between devices: 98.4 us -> none  [shards(): lax.all_gather(jnp.concatenate([pp, ca], axis=1), ROW, axis=0, tiled=True)]
    all_to_all x1, blocking collectives: 47.8 us -> 41.2 us  [shards(): got = lax.all_to_all(part, COL, 0, 0, tiled=True)]
    another operation x0 -> x1, local copies, waits for them, and re-layouts: none -> 6.12 us  [shards(): jnp.stack([jnp.concatenate([pp, ca], axis=1)] * lax.axis_size(ROW))]
  transfers between devices with their start and end apart: 3 -> 2, of which waited for: 3 -> 2; matrix products, arithmetic and copies ran while one was open for 2% -> 1% of each run, Pallas kernels for 0% -> 0%
where the time goes in v1:
time: 437 us
  blocking collectives  361 us (83%)
  matrix products  29.2 us (7%)
  local copies, waits for them, and re-layouts  15.9 us (4%)
  waiting for transfers between devices  14.8 us (3%)
  starting transfers between devices  9.24 us (2%)
  other arithmetic  5.67 us (1%)
    all_to_all x1, blocking collectives, shards(): lax.all_to_all(jnp.stack([jnp.concatenate([pp, ca], axis=1)] * lax.axis_s...  289 us
    all_to_all x1, blocking collectives, shards(): got = lax.all_to_all(part, COL, 0, 0, tiled=True)  41.2 us
    all_to_all x1, blocking collectives, shards(): x = lax.all_to_all(x, ROW, 0, 0, tiled=True)  31.1 us
    dot_general x9, matrix products, dot(): lax.dot_general(a, b, (((ca,), (cb,)), ((), ())), preferred_element_type=...  29.2 us
    all_to_all x1, waiting for transfers between devices, shards(): t = lax.all_to_all(t, ROW, 0, 0, tiled=True)  12.8 us
  transfers between devices with their start and end apart: 2, of which 2 were waited for; matrix products, arithmetic and copies ran while one was open for 1% of the time, Pallas kernels for 0%

profile of v1, /device:TPU:1, one launch (start us, length us, event | category | flops | bytes accessed | tf_op | source)
XLA Modules:
  0.0 436.8 jit_solution(10218395605267237041)
XLA Ops:
  0.6 0.0 copy-start
  0.6 1.2 pad_maximum_fusion
  1.8 0.0 slice-start
  1.9 6.1 %stack.24 = bf16[32,96,2048]{2,1,0:T(8,128)(2,1)} broadcast(bf16[96,2048]{1,0:T(8,128)(2,1)S(1)} %pad_maximum_fusion), dimensions={1,2} | broadcast | bytes 12976128 | tf_op jit(solution)/shard_map/stack | solution.py:25
  8.0 288.7 %all_to_all.25 = bf16[32,96,2048]{2,1,0:T(8,128)(2,1)S(1)} all-to-all(bf16[32,96,2048]{2,1,0:T(8,128)(2,1)} %stack.24), channel_id=1, replica_groups=mesh['x'=4,'zh'=4,'core'=2,'y'=4,'zl'=2] {'x','zh','core'}, dimensions={0} | all-to-all | bytes 25165824 | tf_op jit(solution)/shard_map/all_to_all | solution.py:24
  296.7 0.0 slice-done
  296.7 10.1 %fusion.2 = bf16[2048,768]{0,1:T(8,128)(2,1)S(1)} fusion(bf16[3072,2048]{1,0:T(8,128)(2,1)S(1)} %bitcast.57, bf16[768,1,3072]{2,0,1:T(8,128)(2,1)S(1)} %bitcast.68), kind=kOutput, calls=%fused_computation.3 | convolution fusion | flops 9665249280 | bytes 20447232 | tf_op jit(solution)/shard_map/dot_general | solution.py:14
  306.9 41.2 %all_to_all.26 = bf16[8,96,2048]{2,1,0:T(8,128)(2,1)S(1)} all-to-all(bf16[8,96,2048]{2,1,0:T(8,128)(2,1)S(1)} %bitcast.60), channel_id=1, replica_groups=mesh['x'=4,'zh'=4,'core'=2,'y'=4,'zl'=2] {'y','zl'}, dimensions={0} | all-to-all | bytes 6291456 | tf_op jit(solution)/shard_map/all_to_all | solution.py:30
  348.1 0.6 convert_reduce_fusion
  348.7 0.0 copy-done
  348.7 1.3 fusion.9
  350.0 0.2 copy.30
  350.2 0.2 copy.31
  350.3 0.2 copy.29
  350.5 0.2 maximum_bitcast_fusion.1
  350.7 0.1 copy.32
  350.8 31.1 %all_to_all.27 = bf16[32,3,32,96]{3,2,1,0:T(8,128)(2,1)S(1)} all-to-all(bf16[32,3,32,96]{3,2,1,0:T(8,128)(2,1)S(1)} %copy.32), channel_id=1, replica_groups=mesh['x'=4,'zh'=4,'core'=2,'y'=4,'zl'=2] {'x','zh','core'}, dimensions={0} | all-to-all | bytes 1179648 | tf_op jit(solution)/shard_map/all_to_all | solution.py:39
  381.9 0.3 copy.33
  382.2 1.1 reshape.50
  383.3 6.7 %fusion.19 = f32[96,2048]{1,0:T(8,128)S(1)} fusion(bf16[96,3072]{1,0:T(8,128)(2,1)S(1)} %reshape.50, bf16[3072,2048]{1,0:T(8,128)(2,1)} %bitcast.58), kind=kOutput, calls=%fused_computation.37 | convolution fusion | flops 1207959552 | bytes 13959168 | tf_op jit(solution)/shard_map/dot_general | solution.py:14
  390.0 0.9 copy-done.2
  390.8 0.5 convolution_add_fusion
  391.3 1.0 copy.39
  392.3 1.0 copy.40
  393.3 1.3 maximum_bitcast_fusion
  394.6 1.1 reshape.51
  395.8 5.8 %all-to-all-start.3 = ((f32[32,1,2048]{2,1,0:T(1,128)}), f32[32,1,2048]{2,1,0:T(1,128)S(1)}, u32[]{:S(2)}, u32[]{:S(2)}) async-start(f32[32,1,2048]{2,1,0:T(1,128)} %reshape.51), calls=%async_computation.3 | async-start | bytes 524288 | tf_op jit(solution)/shard_map/all_to_all | solution.py:49
  401.6 12.8 %all-to-all-done.3 = f32[32,1,2048]{2,1,0:T(1,128)S(1)} async-done(((f32[32,1,2048]{2,1,0:T(1,128)}), f32[32,1,2048]{2,1,0:T(1,128)S(1)}, u32[]{:S(2)}, u32[]{:S(2)}) %all-to-all-start.3) | async-done | bytes 262176 | tf_op jit(solution)/shard_map/all_to_all | solution.py:49
  414.3 0.5 broadcast.2
  414.9 1.3 reduce
  416.1 0.3 reshape.52
  416.5 0.9 fusion.17
  417.4 0.3 copy.37
  417.7 0.2 squeeze.12
  417.9 1.0 fusion.18
  419.0 0.3 copy.36
  419.3 0.3 stack.32
  419.6 0.1 maximum_bitcast_fusion.2
  419.7 0.8 copy.38
  420.5 3.5 all-to-all-start.4
  423.9 0.0 copy-start.3
  423.9 2.3 fusion.6
  426.3 3.7 convolution_convert_fusion
  430.0 2.1 all-to-all-done.4
  432.1 0.1 reduce_sum.19
  432.2 2.3 convolution_add_fusion.2
  434.5 1.0 convolution_subtract_fusion
  435.5 1.3 fusion.5
  (17 shorter events, 0.1 us)
Async XLA Ops:
  0.6 348.1 %copy-start = (bf16[1024,1024]{1,0:T(8,128)(2,1)S(1)}, bf16[1024,1024]{1,0:T(8,128)(2,1)}, u32[]{:S(2)}) copy-start(bf16[1024,1024]{1,0:T(8,128)(2,1)} %param.10) | copy-start | bytes 6291460
  1.8 294.9 %slice-start = ((s8[4718592]{0:T(1024)(128)(4,1)}), s8[524288]{0:T(1024)(128)(4,1)S(1)}, s32[]{:S(2)}) async-start(s8[4718592]{0:T(1024)(128)(4,1)} %bitcast.67), calls=%async_computation.5 | async-start | bytes 1048576
  8.0 288.7 %slice-start.1 = ((s8[4718592]{0:T(1024)(128)(4,1)}), s8[4194304]{0:T(1024)(128)(4,1)S(1)}, s32[]{:S(2)}) async-start(s8[4718592]{0:T(1024)(128)(4,1)} %bitcast.67), calls=%async_computation.6 | async-start | bytes 8388608
  296.7 10.2 %copy-start.1 = (bf16[32,96,2048]{2,1,0:T(8,128)(2,1)}, bf16[32,96,2048]{2,1,0:T(8,128)(2,1)S(1)}, u32[]{:S(2)}) copy-start(bf16[32,96,2048]{2,1,0:T(8,128)(2,1)S(1)} %all_to_all.25) | copy-start | bytes 37748740
  389.9 0.9 copy-start.2
  395.8 18.6 %all-to-all-start.3 = ((f32[32,1,2048]{2,1,0:T(1,128)}), f32[32,1,2048]{2,1,0:T(1,128)S(1)}, u32[]{:S(2)}, u32[]{:S(2)}) async-start(f32[32,1,2048]{2,1,0:T(1,128)} %reshape.51), calls=%async_computation.3 | async-start | bytes 524288 | tf_op jit(solution)/shard_map/all_to_all | solution.py:49
  417.4 1.6 copy-start.5
  420.5 11.6 %all-to-all-start.4 = ((f32[8,3,4,1024]{3,2,1,0:T(4,128)}), f32[8,3,4,1024]{3,2,1,0:T(4,128)S(1)}, u32[]{:S(2)}, u32[]{:S(2)}) async-start(f32[8,3,4,1024]{3,2,1,0:T(4,128)} %copy.38), calls=%async_computation.4 | async-start | bytes 786432 | tf_op jit(solution)/shard_map/all_to_all | solution.py:52
  423.9 2.3 copy-start.3
  432.2 3.3 copy-start.4
  434.5 2.3 copy-start.6
